TPU v7x, 256 devices: a whole 4x4x8 slice. The times are simulated.
256 devices in a mesh: task: 16 (over z_lo, y, core), rows: 16 (over z_hi, x).
Axes of the slice: x: 4, y: 4, z: 8 (z_hi: 4, z_lo: 2; z = z_hi * 2 + z_lo), core: 2. Of those that a mesh axis runs over, the one named last changes fastest.
Arguments:
- probes: bfloat16 [16, 384, 8192], P('task', None, 'rows'), may hold values from -48 to 48
- task_weights: bfloat16 [16, 8192, 128], P('task', 'rows'), may hold values from -6 to 6
Outputs:
- merged: float32 [8192, 128], P(('rows', 'task'))
- residual: float32 [8192, 128], P(('rows', 'task'))
All inputs are finite; a program needn't handle non-finite values.
Results may differ from a plain program's by a relative error of at most 0.0003.
Values may be sent and summed in bfloat16 or wider, within the bound.
No kernel may reach another device: no remote copies, remote signals or barrier semaphores. Data moves between devices by JAX's collectives and lax.ppermute only.
A program may use at most 128 MiB of HBM per device.

v0:
```python
import jax
import jax.numpy as jnp
from jax import lax
from jax.sharding import PartitionSpec as P

PROBE = 384
ITERS = 2
ALPHA = 0.9
EPS = 1e-06


def column_squares(vector):
    return lax.psum(jnp.sum(vector * vector, axis=0), ("task", "rows"))


def on_device(probes, task_weights):
    local_x = probes[0]
    local_w = task_weights[0]
    tasks = lax.axis_size("task")
    width = local_x.shape[1]
    share = width // tasks
    cols = local_w.shape[1]
    offset = lax.axis_index("rows") * width
    scale = 1.0 / (PROBE * tasks)
    exact_x = local_x.astype(jnp.float32)
    diag_local = jnp.sum(exact_x * exact_x, axis=0)
    partial_value = jnp.dot(local_x, local_w, preferred_element_type=jnp.float32)
    outputs = lax.psum(partial_value, "rows")
    b_term = ALPHA * jnp.einsum("pd,pc->dc", exact_x, outputs, precision=lax.Precision.HIGHEST)
    b_term = scale * (b_term + (1.0 - ALPHA) * diag_local[:, None] * local_w.astype(jnp.float32))
    raw = jnp.einsum(
        "pd,pe->de",
        local_x,
        lax.all_gather(local_x, "rows", axis=1, tiled=True),
        preferred_element_type=jnp.float32,
    )
    g_term = ALPHA * scale * raw
    square = lax.dynamic_slice_in_dim(g_term, offset, width, 1)
    square = square + jnp.diag((1.0 - ALPHA) * scale * diag_local)
    g_term = lax.dynamic_update_slice_in_dim(g_term, square, offset, 1)
    system, targets = (
        lax.psum_scatter(g_term, "task", scatter_dimension=0, tiled=True),
        lax.psum_scatter(b_term, "task", scatter_dimension=0, tiled=True),
    )
    merged = jnp.zeros((share, cols), jnp.float32)
    residual = targets
    direction = targets
    norm_now = column_squares(residual)
    for step in range(ITERS):
        block = lax.all_gather(direction, "task", axis=0, tiled=True)
        image = jnp.dot(
            system,
            lax.all_gather(block, "rows", axis=0, tiled=True),
            precision=lax.Precision.HIGHEST,
            preferred_element_type=jnp.float32,
        )
        curve = lax.psum(jnp.sum(direction * image, axis=0), ("task", "rows"))
        alpha = norm_now / curve
        merged = merged + alpha * direction
        residual = residual - alpha * image
        norm_next = column_squares(residual)
        direction = residual + norm_next / (norm_now + EPS) * direction
        norm_now = norm_next
    return (merged, residual)


def solution(mesh):
    in_specs = (P("task", None, "rows"), P("task", "rows", None))
    out_specs = (P(("rows", "task"), None), P(("rows", "task"), None))
    return jax.shard_map(
        on_device, mesh=mesh, in_specs=in_specs, out_specs=out_specs, check_vma=False
    )
```

profile of v0, /device:TPU:1, one launch (start us, length us, event | category | flops | bytes accessed | tf_op | source)
XLA Modules:
  0.0 856.5 jit_solution(6923377379118053543)
XLA Ops:
  7.2 0.0 all-reduce.3.cloned.1.call-start
  7.2 2.0 fusion.6
  9.2 0.0 all-reduce.3.cloned.1.call-update
  9.2 0.0 reduce-scatter.7.cloned.1.call-start
  9.2 1.1 multiply_reduce_fusion
  10.4 1.0 copy.11
  11.4 152.3 %all-reduce.3.cloned.1.call-done = f32[384,128]{1,0:T(8,128)} async-done(((f32[384,128]{1,0:T(8,128)}), f32[384,128]{1,0:T(8,128)}) %all-reduce.3.cloned.1.call-update) | async-done | bytes 196624 | tf_op jit(solution)/shard_map/psum | solution.py:28
  163.7 1.5 fusion.3
  165.2 0.8 copy.17
  166.0 0.0 reduce-scatter.7.cloned.1.call-update
  166.1 0.0 all-gather.9.cloned.1.call-start
  166.1 0.7 all-gather.9.cloned.1.call-update
  166.8 0.0 all-gather.5.cloned.1.call-start
  166.8 68.9 %reduce-scatter.7.cloned.1.call-done = f32[32,128]{1,0:T(8,128)} async-done(((f32[512,128]{1,0:T(8,128)}), f32[32,128]{1,0:T(8,128)}) %reduce-scatter.7.cloned.1.call-update) | async-done | bytes 16400 | tf_op jit(solution)/shard_map/reduce_scatter | solution.py:43
  235.7 22.1 %all_gather.16 = f32[512,128]{1,0:T(8,128)} all-gather(f32[32,128]{1,0:T(8,128)} %reduce-scatter.7.cloned.1.call-done), channel_id=1, replica_groups=mesh['task'=16,'rows'=16] {'task'}, dimensions={0}, use_global_device_ids=true | all-gather | bytes 278528 | tf_op jit(solution)/shard_map/all_gather | solution.py:50
  257.8 0.0 all-gather.5.cloned.1.call-update
  257.9 0.0 reduce-scatter.5.cloned.1.call-start
  257.9 84.4 %all-gather.9.cloned.1.call-done = bf16[1,384,8192]{2,1,0:T(8,128)(2,1)} async-done(((bf16[1,384,512]{2,1,0:T(8,128)(2,1)}), bf16[1,384,8192]{2,1,0:T(8,128)(2,1)}) %all-gather.9.cloned.1.call-update) | async-done | bytes 6291472 | tf_op jit(solution)/shard_map/all_gather | solution.py:34
  342.3 13.2 %convolution_multiply_fusion = f32[512,8192]{1,0:T(8,128)} fusion(bf16[1,384,8192]{2,1,0:T(8,128)(2,1)} %all-gather.9.cloned.1.call-done, bf16[1,384,512]{2,1,0:T(8,128)(2,1)} %param.2), kind=kOutput, calls=%fused_computation | convolution fusion | flops 3225419776 | bytes 23461888 | tf_op jit(solution)/shard_map/pd,pe->de/dot_general | solution.py:31
  355.5 2.4 add_dynamic-update-slice_fusion
  357.9 0.0 copy-start.1
  357.9 0.0 reduce-scatter.5.cloned.1.call-update
  358.0 0.0 all-gather.7.cloned.1.call-start
  358.0 0.6 copy-done.1
  358.7 0.1 copy.18
  358.8 0.1 multiply_reduce_fusion.1
  358.9 59.2 %all-gather.5.cloned.1.call-done = f32[8192,128]{1,0:T(8,128)} async-done(((f32[512,128]{1,0:T(8,128)}), f32[8192,128]{1,0:T(8,128)}) %all-gather.5.cloned.1.call-update) | async-done | bytes 4194320 | tf_op jit(solution)/shard_map/all_gather | solution.py:53
  418.1 102.8 %reduce-scatter.5.cloned.1.call-done = f32[32,8192]{1,0:T(8,128)} async-done(((f32[512,8192]{1,0:T(8,128)}), f32[32,8192]{1,0:T(8,128)}) %reduce-scatter.5.cloned.1.call-update) | async-done | bytes 1048592 | tf_op jit(solution)/shard_map/reduce_scatter | solution.py:42
  520.8 0.0 copy-start
  520.8 4.9 multiply_reduce_fusion.4
  525.7 77.6 %all-reduce = (f32[128]{0:T(128)S(1)}, f32[128]{0:T(128)S(1)}) all-reduce(f32[128]{0:T(128)S(1)} %multiply_reduce_fusion.1, f32[128]{0:T(128)S(1)} %get-tuple-element.10), channel_id=1, replica_groups=mesh['task'=16,'rows'=16] {'task','rows'}, use_global_device_ids=true, to_apply=%region_4.5 | all-reduce | flops 256 | bytes 2048 | tf_op jit(solution)/shard_map/psum | solution.py:13
  603.4 73.2 %psum.38 = f32[128]{0:T(128)S(1)} all-reduce(f32[128]{0:T(128)S(1)} %multiply_reduce_fusion.3), channel_id=1, replica_groups=mesh['task'=16,'rows'=16] {'task','rows'}, use_global_device_ids=true, to_apply=%region_9.10 | all-reduce | flops 128 | bytes 1024 | tf_op jit(solution)/shard_map/psum | solution.py:13
  676.5 21.1 %all_gather.18 = f32[512,128]{1,0:T(8,128)} all-gather(f32[32,128]{1,0:T(8,128)S(1)} %multiply_add_fusion.1), channel_id=1, replica_groups=mesh['task'=16,'rows'=16] {'task'}, dimensions={0}, use_global_device_ids=true | all-gather | bytes 278528 | tf_op jit(solution)/shard_map/all_gather | solution.py:50
  697.6 0.0 all-gather.7.cloned.1.call-update
  697.7 68.8 %all-gather.7.cloned.1.call-done = f32[8192,128]{1,0:T(8,128)} async-done(((f32[512,128]{1,0:T(8,128)}), f32[8192,128]{1,0:T(8,128)}) %all-gather.7.cloned.1.call-update) | async-done | bytes 4194320 | tf_op jit(solution)/shard_map/all_gather | solution.py:53
  766.5 0.0 copy-done
  766.5 4.0 multiply_reduce_fusion.2
  770.5 78.4 %psum.39 = f32[128]{0:T(128)S(1)} all-reduce(f32[128]{0:T(128)S(1)} %get-tuple-element.12), channel_id=1, replica_groups=mesh['task'=16,'rows'=16] {'task','rows'}, use_global_device_ids=true, to_apply=%region_11.12 | all-reduce | flops 128 | bytes 1024 | tf_op jit(solution)/shard_map/psum | solution.py:57
  849.0 0.6 multiply_subtract_fusion
  (6 shorter events, 0.1 us)
Async XLA Ops:
  7.2 156.5 %all-reduce.3.cloned.1.call-start = ((), (), s32[]{:S(2)}) async-start(), calls=%async_computation.2 | async-start | bytes 393216 | tf_op jit(solution)/shard_map/psum | solution.py:28
  9.2 226.5 %reduce-scatter.7.cloned.1.call-start = ((), (), s32[]{:S(2)}) async-start(), calls=%async_computation.7 | async-start | bytes 278528 | tf_op jit(solution)/shard_map/reduce_scatter | solution.py:43
  166.1 176.3 %all-gather.9.cloned.1.call-start = ((), (), s32[]{:S(2)}) async-start(), calls=%async_computation.6 | async-start | bytes 6684672 | tf_op jit(solution)/shard_map/all_gather | solution.py:34
  166.8 251.3 %all-gather.5.cloned.1.call-start = ((), (), s32[]{:S(2)}) async-start(), calls=%async_computation.4 | async-start | bytes 4456448 | tf_op jit(solution)/shard_map/all_gather | solution.py:53
  257.9 263.0 %reduce-scatter.5.cloned.1.call-start = ((), (), s32[]{:S(2)}) async-start(), calls=%async_computation.3 | async-start | bytes 17825792 | tf_op jit(solution)/shard_map/reduce_scatter | solution.py:42
  357.9 0.7 copy-start.1
  358.0 408.5 %all-gather.7.cloned.1.call-start = ((), (), s32[]{:S(2)}) async-start(), calls=%async_computation.5 | async-start | bytes 4456448 | tf_op jit(solution)/shard_map/all_gather | solution.py:53
  520.8 245.6 %copy-start = (f32[32,8192]{1,0:T(8,128)S(1)}, f32[32,8192]{1,0:T(8,128)}, u32[]{:S(2)}) copy-start(f32[32,8192]{1,0:T(8,128)} %reduce-scatter.5.cloned.1.call-done) | copy-start | bytes 3145732
Sparse Core Ops, SparseCore 0:
  10.6 153.0 all-reduce.2
  166.2 69.4 reduce-scatter.6
  238.1 104.1 all-gather.8
  344.6 73.4 all-gather.4
  420.5 100.3 reduce-scatter.4
  697.8 68.6 all-gather.6
where the time goes:
time: 857 us; the launch traced here: 856 us
  waiting for transfers between devices  537 us (63%)
  blocking collectives  272 us (32%)
  matrix products  25.6 us (3%)
  between operations  14.2 us (2%)
    psum x1, waiting for transfers between devices, on_device(): outputs = lax.psum(partial_value, 'rows')  152 us
    psum x2, blocking collectives, column_squares(): return lax.psum(jnp.sum(vector * vector, axis=0), ('task', 'rows'))  151 us
    all_gather x2, waiting for transfers between devices, on_device(): lax.all_gather(block, 'rows', axis=0, tiled=True)  128 us
    reduce_scatter x1, waiting for transfers between devices, on_device(): lax.psum_scatter(g_term, 'task', scatter_dimension=0, tiled=True)  103 us
    all_gather x1, waiting for transfers between devices, on_device(): lax.all_gather(local_x, 'rows', axis=1, tiled=True)  84.4 us
    psum x1, blocking collectives, on_device(): curve = lax.psum(jnp.sum(direction * image, axis=0), ('task', 'rows'))  78.4 us
    reduce_scatter x1, waiting for transfers between devices, on_device(): lax.psum_scatter(b_term, 'task', scatter_dimension=0, tiled=True)  68.9 us
    all_gather x2, blocking collectives, on_device(): block = lax.all_gather(direction, 'task', axis=0, tiled=True)  43.2 us
  transfers between devices with their start and end apart: 6, of which 6 were waited for; matrix products, arithmetic and copies ran while one was open for 2% of the time, Pallas kernels for 0%

commit v1 on v0

--- a/solution.py
+++ b/solution.py
@@ -25,7 +25,7 @@
     exact_x = local_x.astype(jnp.float32)
     diag_local = jnp.sum(exact_x * exact_x, axis=0)
     partial_value = jnp.dot(local_x, local_w, preferred_element_type=jnp.float32)
-    outputs = lax.psum(partial_value, "rows")
+    outputs = jnp.sum(lax.all_gather(partial_value, "rows"), axis=0)
     b_term = ALPHA * jnp.einsum("pd,pc->dc", exact_x, outputs, precision=lax.Precision.HIGHEST)
     b_term = scale * (b_term + (1.0 - ALPHA) * diag_local[:, None] * local_w.astype(jnp.float32))
     raw = jnp.einsum(

time: 857 us -> 766 us (0.89)
  waiting for transfers between devices: 537 us -> 447 us
    psum x1 -> x0, waiting for transfers between devices: 152 us -> none  [on_device(): outputs = lax.psum(partial_value, 'rows')]
    all_gather x0 -> x1, waiting for transfers between devices: none -> 70.1 us  [on_device(): outputs = jnp.sum(lax.all_gather(partial_value, 'rows'), axis=0)]
    reduce_scatter x1, waiting for transfers between devices: 68.9 us -> 58.1 us  [on_device(): lax.psum_scatter(b_term, 'task', scatter_dimension=0, tiled=True)]
where the time goes in v1:
time: 766 us
  waiting for transfers between devices  447 us (58%)
  blocking collectives  272 us (36%)
  matrix products  23.2 us (3%)
  between operations  14.2 us (2%)
    psum x2, blocking collectives, column_squares(): return lax.psum(jnp.sum(vector * vector, axis=0), ('task', 'rows'))  151 us
    all_gather x2, waiting for transfers between devices, on_device(): lax.all_gather(block, 'rows', axis=0, tiled=True)  130 us
    reduce_scatter x1, waiting for transfers between devices, on_device(): lax.psum_scatter(g_term, 'task', scatter_dimension=0, tiled=True)  103 us
    all_gather x1, waiting for transfers between devices, on_device(): lax.all_gather(local_x, 'rows', axis=1, tiled=True)  84.6 us
    psum x1, blocking collectives, on_device(): curve = lax.psum(jnp.sum(direction * image, axis=0), ('task', 'rows'))  78.5 us
    all_gather x1, waiting for transfers between devices, on_device(): outputs = jnp.sum(lax.all_gather(partial_value, 'rows'), axis=0)  70.1 us
    reduce_scatter x1, waiting for transfers between devices, on_device(): lax.psum_scatter(b_term, 'task', scatter_dimension=0, tiled=True)  58.1 us
    all_gather x2, blocking collectives, on_device(): block = lax.all_gather(direction, 'task', axis=0, tiled=True)  43.2 us
  transfers between devices with their start and end apart: 6, of which 6 were waited for; matrix products, arithmetic and copies ran while one was open for 2% of the time, Pallas kernels for 0%

profile of v1, /device:TPU:1, one launch (start us, length us, event | category | flops | bytes accessed | tf_op | source)
XLA Modules:
  0.0 765.7 jit_solution(10110276740427094737)
XLA Ops:
  7.2 0.0 copy-start
  7.2 0.0 all-gather.11.cloned.1.call-start
  7.2 2.0 fusion.6
  9.2 0.0 all-gather.11.cloned.1.call-update
  9.3 0.0 reduce-scatter.7.cloned.1.call-start
  9.3 1.0 copy.11
  10.3 1.1 multiply_reduce_fusion
  11.4 70.1 %all-gather.11.cloned.1.call-done = f32[6144,128]{1,0:T(8,128)} async-done(((f32[384,128]{1,0:T(8,128)}), f32[6144,128]{1,0:T(8,128)}) %all-gather.11.cloned.1.call-update) | async-done | bytes 3145744 | tf_op jit(solution)/shard_map/all_gather | solution.py:28
  81.5 2.1 reduce_sum.54
  83.6 1.4 fusion.3
  85.0 0.8 copy.17
  85.8 0.0 reduce-scatter.7.cloned.1.call-update
  85.9 0.0 all-gather.13.cloned.1.call-start
  85.9 0.7 all-gather.13.cloned.1.call-update
  86.6 0.0 all-gather.7.cloned.1.call-start
  86.6 58.1 %reduce-scatter.7.cloned.1.call-done = f32[32,128]{1,0:T(8,128)} async-done(((f32[512,128]{1,0:T(8,128)}), f32[32,128]{1,0:T(8,128)}) %reduce-scatter.7.cloned.1.call-update) | async-done | bytes 16400 | tf_op jit(solution)/shard_map/reduce_scatter | solution.py:43
  144.7 22.1 %all_gather.24 = f32[512,128]{1,0:T(8,128)} all-gather(f32[32,128]{1,0:T(8,128)} %reduce-scatter.7.cloned.1.call-done), channel_id=1, replica_groups=mesh['task'=16,'rows'=16] {'task'}, dimensions={0}, use_global_device_ids=true | all-gather | bytes 278528 | tf_op jit(solution)/shard_map/all_gather | solution.py:50
  166.9 0.0 all-gather.7.cloned.1.call-update
  166.9 0.0 reduce-scatter.5.cloned.1.call-start
  166.9 84.6 %all-gather.13.cloned.1.call-done = bf16[1,384,8192]{2,1,0:T(8,128)(2,1)} async-done(((bf16[1,384,512]{2,1,0:T(8,128)(2,1)}), bf16[1,384,8192]{2,1,0:T(8,128)(2,1)}) %all-gather.13.cloned.1.call-update) | async-done | bytes 6291472 | tf_op jit(solution)/shard_map/all_gather | solution.py:34
  251.5 0.0 copy-done
  251.5 10.9 %convolution_multiply_fusion = f32[512,8192]{1,0:T(8,128)} fusion(bf16[1,384,8192]{2,1,0:T(8,128)(2,1)} %all-gather.13.cloned.1.call-done, bf16[1,384,512]{2,1,0:T(8,128)(2,1)S(1)} %copy-done), kind=kOutput, calls=%fused_computation | convolution fusion | flops 3225419776 | bytes 23461888 | tf_op jit(solution)/shard_map/pd,pe->de/dot_general | solution.py:31
  262.4 2.4 add_dynamic-update-slice_fusion
  264.8 0.0 copy-start.2
  264.8 0.0 reduce-scatter.5.cloned.1.call-update
  264.8 0.0 all-gather.9.cloned.1.call-start
  264.9 0.6 copy-done.2
  265.5 0.1 copy.18
  265.6 0.1 multiply_reduce_fusion.1
  265.7 61.6 %all-gather.7.cloned.1.call-done = f32[8192,128]{1,0:T(8,128)} async-done(((f32[512,128]{1,0:T(8,128)}), f32[8192,128]{1,0:T(8,128)}) %all-gather.7.cloned.1.call-update) | async-done | bytes 4194320 | tf_op jit(solution)/shard_map/all_gather | solution.py:53
  327.3 102.8 %reduce-scatter.5.cloned.1.call-done = f32[32,8192]{1,0:T(8,128)} async-done(((f32[512,8192]{1,0:T(8,128)}), f32[32,8192]{1,0:T(8,128)}) %reduce-scatter.5.cloned.1.call-update) | async-done | bytes 1048592 | tf_op jit(solution)/shard_map/reduce_scatter | solution.py:42
  430.1 0.0 copy-start.1
  430.1 4.9 multiply_reduce_fusion.4
  434.9 77.6 %all-reduce = (f32[128]{0:T(128)S(1)}, f32[128]{0:T(128)S(1)}) all-reduce(f32[128]{0:T(128)S(1)} %multiply_reduce_fusion.1, f32[128]{0:T(128)S(1)} %get-tuple-element.10), channel_id=1, replica_groups=mesh['task'=16,'rows'=16] {'task','rows'}, use_global_device_ids=true, to_apply=%region_4.5 | all-reduce | flops 256 | bytes 2048 | tf_op jit(solution)/shard_map/psum | solution.py:13
  512.6 73.2 %psum.30 = f32[128]{0:T(128)S(1)} all-reduce(f32[128]{0:T(128)S(1)} %multiply_reduce_fusion.3), channel_id=1, replica_groups=mesh['task'=16,'rows'=16] {'task','rows'}, use_global_device_ids=true, to_apply=%region_9.10 | all-reduce | flops 128 | bytes 1024 | tf_op jit(solution)/shard_map/psum | solution.py:13
  585.8 21.1 %all_gather.26 = f32[512,128]{1,0:T(8,128)} all-gather(f32[32,128]{1,0:T(8,128)S(1)} %multiply_add_fusion.1), channel_id=1, replica_groups=mesh['task'=16,'rows'=16] {'task'}, dimensions={0}, use_global_device_ids=true | all-gather | bytes 278528 | tf_op jit(solution)/shard_map/all_gather | solution.py:50
  606.9 0.0 all-gather.9.cloned.1.call-update
  606.9 68.8 %all-gather.9.cloned.1.call-done = f32[8192,128]{1,0:T(8,128)} async-done(((f32[512,128]{1,0:T(8,128)}), f32[8192,128]{1,0:T(8,128)}) %all-gather.9.cloned.1.call-update) | async-done | bytes 4194320 | tf_op jit(solution)/shard_map/all_gather | solution.py:53
  675.7 0.0 copy-done.1
  675.7 4.0 multiply_reduce_fusion.2
  679.8 78.5 %psum.31 = f32[128]{0:T(128)S(1)} all-reduce(f32[128]{0:T(128)S(1)} %get-tuple-element.12), channel_id=1, replica_groups=mesh['task'=16,'rows'=16] {'task','rows'}, use_global_device_ids=true, to_apply=%region_11.12 | all-reduce | flops 128 | bytes 1024 | tf_op jit(solution)/shard_map/psum | solution.py:57
  758.2 0.6 multiply_subtract_fusion
  (6 shorter events, 0.1 us)
Async XLA Ops:
  7.2 244.4 %copy-start = (bf16[1,384,512]{2,1,0:T(8,128)(2,1)S(1)}, bf16[1,384,512]{2,1,0:T(8,128)(2,1)}, u32[]{:S(2)}) copy-start(bf16[1,384,512]{2,1,0:T(8,128)(2,1)} %param.2) | copy-start | bytes 1179652
  7.2 74.3 %all-gather.11.cloned.1.call-start = ((), (), s32[]{:S(2)}) async-start(), calls=%async_computation.5 | async-start | bytes 3342336 | tf_op jit(solution)/shard_map/all_gather | solution.py:28
  9.3 135.5 %reduce-scatter.7.cloned.1.call-start = ((), (), s32[]{:S(2)}) async-start(), calls=%async_computation.7 | async-start | bytes 278528 | tf_op jit(solution)/shard_map/reduce_scatter | solution.py:43
  85.9 165.7 %all-gather.13.cloned.1.call-start = ((), (), s32[]{:S(2)}) async-start(), calls=%async_computation.6 | async-start | bytes 6684672 | tf_op jit(solution)/shard_map/all_gather | solution.py:34
  86.6 240.7 %all-gather.7.cloned.1.call-start = ((), (), s32[]{:S(2)}) async-start(), calls=%async_computation.3 | async-start | bytes 4456448 | tf_op jit(solution)/shard_map/all_gather | solution.py:53
  166.9 263.2 %reduce-scatter.5.cloned.1.call-start = ((), (), s32[]{:S(2)}) async-start(), calls=%async_computation.2 | async-start | bytes 17825792 | tf_op jit(solution)/shard_map/reduce_scatter | solution.py:42
  264.8 0.7 copy-start.2
  264.8 410.9 %all-gather.9.cloned.1.call-start = ((), (), s32[]{:S(2)}) async-start(), calls=%async_computation.4 | async-start | bytes 4456448 | tf_op jit(solution)/shard_map/all_gather | solution.py:53
  430.1 245.7 %copy-start.1 = (f32[32,8192]{1,0:T(8,128)S(1)}, f32[32,8192]{1,0:T(8,128)}, u32[]{:S(2)}) copy-start(f32[32,8192]{1,0:T(8,128)} %reduce-scatter.5.cloned.1.call-done) | copy-start | bytes 3145732
Sparse Core Ops, SparseCore 0:
  10.4 71.0 all-gather.10
  86.0 58.7 reduce-scatter.6
  147.1 104.3 all-gather.12
  253.8 73.4 all-gather.6
  329.7 100.3 reduce-scatter.4
  607.0 68.6 all-gather.8
